TPU v7x, 32 devices: a whole 2x2x4 slice. The times are simulated.
32 devices in a mesh: pair: 8 (over z, core), aux: 4 (over y, x).
Axes of the slice: x: 2, y: 2, z: 4, core: 2. Of those that a mesh axis runs over, the one named last changes fastest.
Arguments:
- factors: bfloat16 [384, 16, 64, 128], P('aux', 'pair'), may hold values from -1.75 to 1.75
- pairs: int32 [80, 2], replicated, may hold values from 0 to 15, as said below
- shared: int32 [80, 4], P(None, 'aux'), may hold values 0 or 1
- owners: int32 [80], replicated, may hold values from 0 to 7, as said below
Outputs:
- exchange_matrix: float32 [16, 128, 2048], P('pair', 'aux')
- pair_tiles: float32 [8, 40, 128, 128], P('pair', None, 'aux')
Inputs may be any that keep to these rules, and one draw needn't show every extreme that they name: Distinct pairs (a, b) with a <= b. `owners`: each device owns at most 40 pairs and one device owns exactly 40.
All inputs are finite; a program needn't handle non-finite values. No bound on the sum of `shared` on one device may be relied on, other than what follows from the above.
Results may differ from a plain program's by a relative error of at most 0.0003.
Values may be sent and summed in bfloat16 or wider, within the bound.
No kernel may reach another device: no remote copies, remote signals or barrier semaphores. Data moves between devices by JAX's collectives and lax.ppermute only.
A program may use at most 128 MiB of HBM per device.

v0:
```python
import jax
import jax.numpy as jnp
from jax import lax
from jax.sharding import PartitionSpec as P


def body(factors, pairs, shared, owners):
    aux_rows, tiles_here, orbitals, tile_width = factors.shape
    owner_count = lax.axis_size("pair")
    tile_count = tiles_here * owner_count
    basis_count = tile_count * tile_width
    pair_count = pairs.shape[0]
    shard_rows = tile_width // lax.axis_size("aux")
    myself = lax.axis_index("pair")
    column = lax.axis_index("aux")
    slot_count = 4 * (pair_count // owner_count)
    pair_ids = jnp.arange(pair_count, dtype=jnp.int32)
    same_owner = owners[:, None] == owners[None, :]
    owner_rank = jnp.sum(
        (same_owner & (pair_ids[None, :] < pair_ids[:, None])).astype(jnp.int32), axis=1
    )
    slot_ids = jnp.arange(slot_count, dtype=jnp.int32)
    matches = (owners[None, :] == myself) & (owner_rank[None, :] == slot_ids[:, None])
    picked = jnp.sum(jnp.where(matches, pair_ids[None, :], 0), axis=1)
    live_slot = jnp.any(matches, axis=1).astype(jnp.float32)
    left_ids = pairs[picked, 0]
    right_ids = pairs[picked, 1]
    weights = live_slot * shared[picked, 0].astype(jnp.float32)
    gathered = lax.all_gather(factors, "pair", axis=1, tiled=True)

    def contract(slot_item):
        left_id, right_id, slot_scale = slot_item
        left_block = lax.dynamic_index_in_dim(gathered, left_id, 1, keepdims=False).reshape(
            aux_rows * orbitals, tile_width
        )
        right_block = lax.dynamic_index_in_dim(gathered, right_id, 1, keepdims=False).reshape(
            aux_rows * orbitals, tile_width
        )
        product = lax.dot_general(
            left_block, right_block, (((0,), (0,)), ((), ())), preferred_element_type=jnp.float32
        )
        return product * slot_scale

    partial_tiles = lax.map(contract, (left_ids, right_ids, weights))
    summed = lax.psum(partial_tiles, "aux")
    direct = lax.dynamic_slice_in_dim(summed, column * shard_rows, shard_rows, 1)
    mirror = lax.dynamic_slice_in_dim(
        jnp.swapaxes(summed, 1, 2), column * shard_rows, shard_rows, 1
    )
    tile_ids = jnp.arange(tile_count, dtype=jnp.int32)
    off_diagonal = live_slot * (left_ids != right_ids).astype(jnp.float32)
    left_hot = (left_ids[:, None] == tile_ids[None, :]).astype(jnp.float32)
    right_hot = (right_ids[:, None] == tile_ids[None, :]).astype(jnp.float32)
    upper_part = jnp.einsum(
        "jt,jc,jrm->trcm",
        left_hot * live_slot[:, None],
        right_hot,
        direct,
        precision=lax.Precision.HIGHEST,
    )
    lower_part = jnp.einsum(
        "jt,jc,jrm->trcm",
        right_hot * off_diagonal[:, None],
        left_hot,
        mirror,
        precision=lax.Precision.HIGHEST,
    )
    contribution = (upper_part + lower_part).reshape(tile_count, shard_rows, basis_count)
    matrix_rows = lax.psum_scatter(contribution, "pair", scatter_dimension=0, tiled=True)
    owned_tiles = direct[None]
    return (matrix_rows, owned_tiles)


def solution(mesh):
    placed = (P("aux", "pair", None, None), P(), P(None, "aux"), P())
    return jax.shard_map(
        body,
        mesh=mesh,
        in_specs=placed,
        out_specs=(P("pair", "aux", None), P("pair", None, "aux", None)),
        check_vma=False,
    )
```

profile of v0, /device:TPU:0, one launch (start us, length us, event | category | flops | bytes accessed | tf_op | source)
XLA Modules:
  0.0 886.8 jit_solution(12804275647070934509)
XLA Ops:
  7.2 4.4 copy.20
  15.7 218.7 %all-gather.2.cloned.1.call-done = bf16[96,16,64,128]{3,2,0,1:T(8,128)(2,1)} async-done(((bf16[96,2,64,128]{3,2,0,1:T(8,128)(2,1)}), bf16[96,16,64,128]{3,2,0,1:T(8,128)(2,1)}) %all-gather.2.cloned.1.call-update) | async-done | bytes 25165840 | tf_op jit(solution)/shard_map/all_gather | solution.py:29
  234.4 26.9 %copy.21 = bf16[96,16,64,128]{3,0,2,1:T(8,128)(2,1)} copy(bf16[96,16,64,128]{3,2,0,1:T(8,128)(2,1)} %all-gather.2.cloned.1.call-done) | data formatting | bytes 50331648 | tf_op jit(solution)/shard_map/while | solution.py:44
  261.3 470.9 %while.10 = (s32[]{:T(128)}, f32[40,128,128]{2,0,1:T(8,128)}, s32[40]{0:T(128)S(1)}, bf16[96,16,64,128]{3,0,2,1:T(8,128)(2,1)}, s32[40]{0:T(128)S(1)}, /*index=5*/f32[40]{0:T(128)S(1)}, s32[]{:T(128)}, s32[]{:T(128)}, s32[]{:T(128)}) while((s32[]{:T(128)}, f32[40,128,128]{2,0,1:T(8,128)}, s32[40]{0:T(128)S(1)}, ...), condition=%wide.region_4.5_spmd, body=%wide.region_3.4_spmd.sunk | while | flops 201342976 | bytes 3343057 | solution.py:44
  266.9 3.1 fusion.42
  278.7 3.1 fusion.42
  290.4 3.1 fusion.42
  302.2 3.1 fusion.42
  313.9 3.1 fusion.42
  325.7 3.1 fusion.42
  337.5 3.1 fusion.42
  349.2 3.1 fusion.42
  361.0 3.2 fusion.42
  364.2 3.0 dynamic_update_slice.5
  372.9 3.1 fusion.42
  376.0 3.0 dynamic_update_slice.5
  384.6 3.1 fusion.42
  387.8 3.0 dynamic_update_slice.5
  396.4 3.1 fusion.42
  399.6 3.0 dynamic_update_slice.5
  408.2 3.1 fusion.42
  411.4 3.0 dynamic_update_slice.5
  420.0 3.1 fusion.42
  423.2 3.0 dynamic_update_slice.5
  431.8 3.2 fusion.42
  435.0 3.0 dynamic_update_slice.5
  443.7 3.1 fusion.42
  446.8 3.0 dynamic_update_slice.5
  455.4 3.1 fusion.42
  467.2 3.1 fusion.42
  479.0 3.1 fusion.42
  490.7 3.1 fusion.42
  502.5 3.1 fusion.42
  514.2 3.1 fusion.42
  526.0 3.2 fusion.42
  537.8 3.1 fusion.42
  549.6 3.1 fusion.42
  561.3 3.1 fusion.42
  573.1 3.1 fusion.42
  584.8 3.1 fusion.42
  596.5 3.1 fusion.42
  608.3 3.1 fusion.42
  620.0 3.1 fusion.42
  631.8 3.1 fusion.42
  643.5 3.1 fusion.42
  646.7 3.0 dynamic_update_slice.5
  655.3 3.1 fusion.42
  658.5 3.0 dynamic_update_slice.5
  667.1 3.1 fusion.42
  670.2 3.0 dynamic_update_slice.5
  678.9 3.1 fusion.42
  682.0 3.0 dynamic_update_slice.5
  690.7 3.1 fusion.42
  693.8 3.0 dynamic_update_slice.5
  702.4 3.2 fusion.42
  705.6 3.0 dynamic_update_slice.5
  714.3 3.1 fusion.42
  726.0 3.1 fusion.42
  732.5 76.4 %all-reduce.4.cloned.1.call-done = f32[40,128,128]{2,0,1:T(8,128)} async-done(((f32[40,128,128]{2,0,1:T(8,128)}), f32[40,128,128]{2,0,1:T(8,128)}) %all-reduce.4.cloned.1.call-update) | async-done | bytes 2621456 | tf_op jit(solution)/shard_map/psum | solution.py:45
  813.7 3.4 fusion.17
  817.2 3.6 add_bitcast_fusion
  820.8 4.4 copy.24
  825.1 4.9 reshape.48
  831.0 49.2 %reduce-scatter.2.cloned.1.call-done = f32[2,32,2048]{2,1,0:T(8,128)} async-done(((f32[16,32,2048]{2,1,0:T(8,128)}), f32[2,32,2048]{2,1,0:T(8,128)}) %reduce-scatter.2.cloned.1.call-update) | async-done | bytes 524304 | tf_op jit(solution)/shard_map/reduce_scatter | solution.py:69
  (179 shorter events, 157.5 us)
Async XLA Ops:
  7.2 5.4 copy-start
  7.2 227.2 %all-gather.2.cloned.1.call-start = ((), (), s32[]{:S(2)}) async-start(), calls=%async_computation.1 | async-start | bytes 28311552 | tf_op jit(solution)/shard_map/all_gather | solution.py:29
  11.6 0.7 copy-start.3
  11.6 3.1 copy-start.2
  11.6 797.3 %all-reduce.4.cloned.1.call-start = ((), (), s32[]{:S(2)}) async-start(), calls=%async_computation.2 | async-start | bytes 5242880 | tf_op jit(solution)/shard_map/psum | solution.py:45
  732.2 148.0 %reduce-scatter.2.cloned.1.call-start = ((), (), s32[]{:S(2)}) async-start(), calls=%async_computation.3 | async-start | bytes 4718592 | tf_op jit(solution)/shard_map/reduce_scatter | solution.py:69
  825.1 55.1 %copy-start.1 = (s32[80,2]{0,1:T(2,128)S(1)}, s32[80,2]{0,1:T(2,128)}, u32[]{:S(2)}) copy-start(s32[80,2]{0,1:T(2,128)} %param.7) | copy-start | bytes 1924
Sparse Core Ops, SparseCore 0:
  11.8 222.5 all-gather.1
  732.3 76.5 all-reduce.3
  830.2 49.9 reduce-scatter.1
where the time goes:
time: 891 us; the launch traced here: 887 us
  waiting for transfers between devices  344 us (39%)
  local copies, waits for them, and re-layouts  239 us (27%)
  loops' own time  156 us (18%)
  matrix products  133 us (15%)
  between operations  13.9 us (2%)
    all_gather x1, waiting for transfers between devices, body(): gathered = lax.all_gather(factors, 'pair', axis=1, tiled=True)  219 us
    another operation x1, loops' own time, body(): partial_tiles = lax.map(contract, (left_ids, right_ids, weights))  156 us
    dot_general x40, matrix products, contract(): lax.dot_general(left_block, right_block, (((0,), (0,)), ((), ())), prefer...  126 us
    dynamic_update_slice x40, local copies, waits for them, and re-layouts, body(): partial_tiles = lax.map(contract, (left_ids, right_ids, weights))  119 us
    psum x1, waiting for transfers between devices, body(): summed = lax.psum(partial_tiles, 'aux')  76.4 us
    dynamic_slice x120, local copies, waits for them, and re-layouts, body(): partial_tiles = lax.map(contract, (left_ids, right_ids, weights))  70.4 us
    reduce_scatter x1, waiting for transfers between devices, body(): lax.psum_scatter(contribution, 'pair', scatter_dimension=0, tiled=True)  49.2 us
    while x1, local copies, waits for them, and re-layouts, body(): partial_tiles = lax.map(contract, (left_ids, right_ids, weights))  26.9 us
  transfers between devices with their start and end apart: 3, of which 3 were waited for; matrix products, arithmetic and copies ran while one was open for 0% of the time, Pallas kernels for 0%

commit v1 on v0

--- a/solution.py
+++ b/solution.py
@@ -2,6 +2,23 @@
 import jax.numpy as jnp
 from jax import lax
 from jax.sharding import PartitionSpec as P
+
+
+def in_order(tiles, dim):
+    tiles = jnp.moveaxis(tiles, 0, dim)
+    shape = tiles.shape
+    return tiles.reshape(*shape[:dim], shape[dim] * shape[dim + 1], *shape[dim + 2 :])
+
+
+def doubled(x, axis):
+    count, here = (lax.axis_size(axis), lax.axis_index(axis))
+    pieces, distance = (x[None], 1)
+    while distance < count:
+        other = lax.ppermute(pieces, axis, [(i, i ^ distance) for i in range(count)])
+        low = here & distance == 0
+        pieces = jnp.concatenate([jnp.where(low, pieces, other), jnp.where(low, other, pieces)])
+        distance *= 2
+    return pieces
 
 
 def body(factors, pairs, shared, owners):
@@ -26,7 +43,7 @@
     left_ids = pairs[picked, 0]
     right_ids = pairs[picked, 1]
     weights = live_slot * shared[picked, 0].astype(jnp.float32)
-    gathered = lax.all_gather(factors, "pair", axis=1, tiled=True)
+    gathered = in_order(doubled(factors, "pair"), 1)
 
     def contract(slot_item):
         left_id, right_id, slot_scale = slot_item

time: 891 us -> 1410 us (1.58)
  waiting for transfers between devices: 344 us -> 807 us
  other arithmetic: 0.45 us -> 56.2 us
    ppermute x0 -> x3, waiting for transfers between devices: none -> 678 us  [doubled(): lax.ppermute(pieces, axis, [(i, i ^ distance) for i in range(count)])]
    all_gather x1 -> x0, waiting for transfers between devices: 219 us -> none  [body(): gathered = lax.all_gather(factors, 'pair', axis=1, tiled=True)]
    transpose x0 -> x1, local copies, waits for them, and re-layouts: none -> 26.9 us  [in_order(): tiles = jnp.moveaxis(tiles, 0, dim)]
    while x1 -> x0, local copies, waits for them, and re-layouts: 26.9 us -> none  [body(): partial_tiles = lax.map(contract, (left_ids, right_ids, weights))]
    select_n x0 -> x3, other arithmetic: none -> 24.8 us  [doubled(): jnp.where(low, pieces, other)]
    transpose x0 -> x1, other arithmetic: none -> 20.5 us  [in_order(): tiles = jnp.moveaxis(tiles, 0, dim)]
  transfers between devices with their start and end apart: 3 -> 5, of which waited for: 3 -> 5; matrix products, arithmetic and copies ran while one was open for 0% -> 0% of each run, Pallas kernels for 0% -> 0%
where the time goes in v1:
time: 1410 us
  waiting for transfers between devices  807 us (57%)
  local copies, waits for them, and re-layouts  235 us (17%)
  loops' own time  156 us (11%)
  matrix products  133 us (9%)
  other arithmetic  56.2 us (4%)
  between operations  14.2 us (1%)
    ppermute x3, waiting for transfers between devices, doubled(): lax.ppermute(pieces, axis, [(i, i ^ distance) for i in range(count)])  678 us
    another operation x1, loops' own time, body(): partial_tiles = lax.map(contract, (left_ids, right_ids, weights))  156 us
    dot_general x40, matrix products, contract(): lax.dot_general(left_block, right_block, (((0,), (0,)), ((), ())), prefer...  126 us
    dynamic_update_slice x40, local copies, waits for them, and re-layouts, body(): partial_tiles = lax.map(contract, (left_ids, right_ids, weights))  118 us
    psum x1, waiting for transfers between devices, body(): summed = lax.psum(partial_tiles, 'aux')  79.2 us
    dynamic_slice x120, local copies, waits for them, and re-layouts, body(): partial_tiles = lax.map(contract, (left_ids, right_ids, weights))  70.4 us
    reduce_scatter x1, waiting for transfers between devices, body(): lax.psum_scatter(contribution, 'pair', scatter_dimension=0, tiled=True)  49.2 us
  transfers between devices with their start and end apart: 5, of which 5 were waited for; matrix products, arithmetic and copies ran while one was open for 0% of the time, Pallas kernels for 0%

profile of v1, /device:TPU:0, one launch (start us, length us, event | category | flops | bytes accessed | tf_op | source)
XLA Modules:
  0.0 1407.2 jit_solution(1579510717877265110)
XLA Ops:
  7.7 5.6 collective-permute-done
  13.4 3.3 broadcast_select_fusion.5
  16.6 3.5 pad_maximum_fusion.1
  23.1 136.1 %collective-permute-done.1 = bf16[2,96,2,64,128]{4,3,2,1,0:T(8,128)(2,1)} collective-permute-done((bf16[2,96,2,64,128]{4,3,2,1,0:T(8,128)(2,1)}, bf16[2,96,2,64,128]{4,3,2,1,0:T(8,128)(2,1)}, u32[]{:S(2)}, u32[]{:S(2)}) %collective-permute-start.1) | collective-permute-done | bytes 6291488 | tf_op jit(solution)/shard_map/ppermute | solution.py:17
  159.2 4.7 broadcast_select_fusion.3
  164.0 6.9 pad_maximum_fusion
  178.4 536.5 %collective-permute-done.2 = bf16[4,96,2,64,128]{4,3,2,1,0:T(8,128)(2,1)} collective-permute-done((bf16[4,96,2,64,128]{4,3,2,1,0:T(8,128)(2,1)}, bf16[4,96,2,64,128]{4,3,2,1,0:T(8,128)(2,1)}, u32[]{:S(2)}, u32[]{:S(2)}) %collective-permute-start.2) | collective-permute-done | bytes 12582944 | tf_op jit(solution)/shard_map/ppermute | solution.py:17
  715.0 16.9 %broadcast_select_fusion.1 = (bf16[4,96,2,64,128]{4,3,2,1,0:T(8,128)(2,1)}, bf16[4,96,2,64,128]{4,3,2,1,0:T(8,128)(2,1)}) fusion(bf16[4,96,2,64,128]{4,3,2,1,0:T(8,128)(2,1)} %collective-permute-done.2, pred[]{:T(512)S(6)} %eq.82, bf16[2,96,2,64,128]{4,3,2,1,0:T(8,128)(2,1)} %copy-done.4, bf16[2,96,2,64,128]{4,3,2,1,0:T(8,128)(2,1)} %copy-done.3), kind=kLoop, calls=%fused_computation.14 | loop fusion | flops 18874368 | bytes 50331648 | tf_op jit(solution)/shard_map/jit(_where)/select_n | solution.py:19
  731.8 20.5 %maximum_bitcast_fusion = bf16[96,8,2,64,128]{4,3,2,0,1:T(8,128)(2,1)} fusion(bf16[4,96,2,64,128]{4,3,2,1,0:T(8,128)(2,1)} %get-tuple-element.48, bf16[4,96,2,64,128]{4,3,2,1,0:T(8,128)(2,1)} %get-tuple-element.47), kind=kLoop, calls=%fused_computation.11 | loop fusion | flops 12582912 | bytes 50331648 | tf_op jit(solution)/shard_map/transpose | solution.py:8
  752.4 26.9 %copy.14 = bf16[96,8,2,64,128]{4,0,3,2,1:T(8,128)(2,1)} copy(bf16[96,8,2,64,128]{4,3,2,0,1:T(8,128)(2,1)} %maximum_bitcast_fusion) | data formatting | bytes 50331648 | tf_op jit(solution)/shard_map/transpose | solution.py:8
  779.2 470.2 %while.10 = (s32[]{:T(128)}, f32[40,128,128]{2,0,1:T(8,128)}, s32[40]{0:T(128)S(1)}, bf16[96,16,64,128]{3,0,2,1:T(8,128)(2,1)}, s32[40]{0:T(128)S(1)}, /*index=5*/f32[40]{0:T(128)S(1)}, s32[]{:T(128)}, s32[]{:T(128)}, s32[]{:T(128)}) while((s32[]{:T(128)}, f32[40,128,128]{2,0,1:T(8,128)}, s32[40]{0:T(128)S(1)}, ...), condition=%wide.region_4.5_spmd, body=%wide.region_3.4_spmd.sunk | while | flops 201342976 | bytes 3343057 | solution.py:61
  784.9 3.1 fusion.42
  796.6 3.1 fusion.42
  808.4 3.1 fusion.42
  820.1 3.1 fusion.42
  831.8 3.1 fusion.42
  843.6 3.1 fusion.42
  855.3 3.1 fusion.42
  867.1 3.1 fusion.42
  878.8 3.2 fusion.42
  890.6 3.1 fusion.42
  902.3 3.1 fusion.42
  914.1 3.1 fusion.42
  925.8 3.1 fusion.42
  937.6 3.1 fusion.42
  949.3 3.1 fusion.42
  961.1 3.1 fusion.42
  972.8 3.1 fusion.42
  976.0 3.0 dynamic_update_slice.5
  984.6 3.1 fusion.42
  987.7 3.0 dynamic_update_slice.5
  996.4 3.1 fusion.42
  999.5 3.0 dynamic_update_slice.5
  1008.2 3.2 fusion.42
  1011.3 3.0 dynamic_update_slice.5
  1020.0 3.1 fusion.42
  1023.1 3.0 dynamic_update_slice.5
  1031.8 3.1 fusion.42
  1034.9 3.0 dynamic_update_slice.5
  1043.5 3.2 fusion.42
  1055.3 3.1 fusion.42
  1058.5 3.0 dynamic_update_slice.5
  1067.1 3.1 fusion.42
  1078.9 3.1 fusion.42
  1090.6 3.1 fusion.42
  1102.4 3.1 fusion.42
  1114.1 3.1 fusion.42
  1125.9 3.1 fusion.42
  1137.6 3.1 fusion.42
  1149.4 3.1 fusion.42
  1161.1 3.1 fusion.42
  1172.9 3.1 fusion.42
  1184.6 3.1 fusion.42
  1196.4 3.1 fusion.42
  1208.1 3.1 fusion.42
  1219.9 3.1 fusion.42
  1231.6 3.1 fusion.42
  1243.4 3.1 fusion.42
  1249.8 79.2 %all-reduce.4.cloned.1.call-done = f32[40,128,128]{2,0,1:T(8,128)} async-done(((f32[40,128,128]{2,0,1:T(8,128)}), f32[40,128,128]{2,0,1:T(8,128)}) %all-reduce.4.cloned.1.call-update) | async-done | bytes 2621456 | tf_op jit(solution)/shard_map/psum | solution.py:62
  1333.8 3.4 fusion.17
  1337.2 3.6 add_bitcast_fusion
  1340.8 4.4 copy.17
  1345.2 4.9 reshape.52
  1351.1 49.2 %reduce-scatter.2.cloned.1.call-done = f32[2,32,2048]{2,1,0:T(8,128)} async-done(((f32[16,32,2048]{2,1,0:T(8,128)}), f32[2,32,2048]{2,1,0:T(8,128)}) %reduce-scatter.2.cloned.1.call-update) | async-done | bytes 524304 | tf_op jit(solution)/shard_map/reduce_scatter | solution.py:86
  (193 shorter events, 185.0 us)
Async XLA Ops:
  7.2 168.2 %copy-start = (s32[80,2]{0,1:T(2,128)S(1)}, s32[80,2]{0,1:T(2,128)}, u32[]{:S(2)}) copy-start(s32[80,2]{0,1:T(2,128)} %param.7) | copy-start | bytes 1924
  7.2 1321.8 %all-reduce.4.cloned.1.call-start = ((), (), s32[]{:S(2)}) async-start(), calls=%async_computation.1 | async-start | bytes 5242880 | tf_op jit(solution)/shard_map/psum | solution.py:62
  7.2 6.1 collective-permute-start
  16.6 3.5 copy-start.5
  20.2 139.1 %collective-permute-start.1 = (bf16[2,96,2,64,128]{4,3,2,1,0:T(8,128)(2,1)}, bf16[2,96,2,64,128]{4,3,2,1,0:T(8,128)(2,1)}, u32[]{:S(2)}, u32[]{:S(2)}) collective-permute-start(bf16[2,96,2,64,128]{4,3,2,1,0:T(8,128)(2,1)} %pad_maximum_fusion.1), channel_id=1, source_target_pairs={{0,8},{4,12},{8,0},{12,4},{16,24},{20,28},{24,16},{28,20},{1,9},{5... | collective-permute-start | bytes 18874376 | tf_op jit(solution)/shard_map/ppermute | solution.py:17
  163.9 7.0 copy-start.3
  163.9 8.3 copy-start.4
  163.9 11.1 copy-start.6
  164.0 13.5 copy-start.2
  172.2 542.7 %collective-permute-start.2 = (bf16[4,96,2,64,128]{4,3,2,1,0:T(8,128)(2,1)}, bf16[4,96,2,64,128]{4,3,2,1,0:T(8,128)(2,1)}, u32[]{:S(2)}, u32[]{:S(2)}) collective-permute-start(bf16[4,96,2,64,128]{4,3,2,1,0:T(8,128)(2,1)} %pad_maximum_fusion), channel_id=1, source_target_pairs={{0,16},{4,20},{8,24},{12,28},{16,0},{20,4},{24,8},{28,12},{1,17},{... | collective-permute-start | bytes 37748744 | tf_op jit(solution)/shard_map/ppermute | solution.py:17
  1249.5 150.8 %reduce-scatter.2.cloned.1.call-start = ((), (), s32[]{:S(2)}) async-start(), calls=%async_computation.2 | async-start | bytes 4718592 | tf_op jit(solution)/shard_map/reduce_scatter | solution.py:86
  1340.8 59.5 %copy-start.1 = (s32[80,2]{0,1:T(2,128)S(1)}, s32[80,2]{0,1:T(2,128)}, u32[]{:S(2)}) copy-start(s32[80,2]{0,1:T(2,128)} %param.7) | copy-start | bytes 1924
Sparse Core Ops, SparseCore 0:
  1249.6 79.3 all-reduce.3
  1350.3 49.9 reduce-scatter.1
